TPU v7x, 256 devices: a whole 4x4x8 slice. The times are simulated.
256 devices in a mesh: seq: 16 (over x, y), resp: 16 (over z, core).
Axes of the slice: x: 4, y: 4, z: 8, core: 2. Of those that a mesh axis runs over, the one named last changes fastest.
Arguments:
- queries: bfloat16 [16, 8192, 1024], P('resp', 'seq'), may hold values from -1.796875 to 1.796875
- keys: bfloat16 [16, 8192, 1024], P('resp', 'seq'), may hold values from -1.796875 to 1.796875
- values: bfloat16 [16, 8192, 1024], P('resp', 'seq'), may hold values from -6 to 6
- grad_out: bfloat16 [16, 8192, 1024], P('resp', 'seq'), may hold values from -6 to 6
- lengths: int32 [15], replicated, may hold values from 8 to 16
Outputs:
- attended: bfloat16 [16, 8192, 1024], P('resp', 'seq')
- grad_queries: bfloat16 [16, 8192, 1024], P('resp', 'seq')
- grad_keys: bfloat16 [16, 8192, 1024], P('resp', 'seq')
- grad_values: bfloat16 [16, 8192, 1024], P('resp', 'seq')
All inputs are finite; a program needn't handle non-finite values.
Results may differ from a plain program's by a relative error of at most 0.005.
Values sent between devices are 32-bit elements; how exact they have to be, the bound alone decides.
A program may use at most 128 MiB of HBM per device.

v0:
```python
import math

import jax
import jax.numpy as jnp
from jax import lax
from jax.sharding import Mesh
from jax.sharding import PartitionSpec as P

HEADS = 8
HEAD = 128
BLOCK = 512
SEQ = ("seq_0", "seq_1")
RESP = ("resp_0", "resp_1")


def filled_with(x, identity):
    return jnp.zeros_like(x) + jnp.asarray(identity, x.dtype)


def carried_in(x, axes, combine, identity, reverse):
    before = start = filled_with(x, identity)
    total = x
    for axis in reversed(axes):
        length, mine = (lax.axis_size(axis), lax.axis_index(axis))
        pieces = lax.all_gather(total, axis)
        inside, total = (start, start)
        for k in reversed(range(length)) if reverse else range(length):
            passed = k > mine if reverse else k < mine
            total = combine(total, pieces[k])
            inside = jnp.where(passed, total, inside)
        before = combine(inside, before)
    return before


def split_up(x, dim, length):
    before, after = (x.shape[:dim], x.shape[dim + 1 :])
    return jnp.moveaxis(x.reshape(*before, length, -1, *after), dim, 0)


def summed_on_arrival(x, axis, dim):
    length = lax.axis_size(axis)
    parts = lax.all_to_all(split_up(x, dim, length), axis, 0, 0, tiled=True)
    return jnp.sum(parts, axis=0)


def sum_in_two_steps(x, axes, dim):
    far, near = axes
    parts = split_up(x, dim, lax.axis_size(far))
    nearer = summed_on_arrival(parts, near, dim + 1)
    arrived = lax.all_to_all(nearer, far, split_axis=0, concat_axis=0, tiled=True)
    return arrived.sum(axis=0)


def filled_up(lines, length):
    spare = -len(lines) % length
    return jnp.pad(lines, [(0, spare)] + [(0, 0)] * (lines.ndim - 1))


def sent_to_all(x, axis):
    copies = jnp.broadcast_to(x, (lax.axis_size(axis), *x.shape))
    return lax.all_to_all(copies, axis, split_axis=0, concat_axis=0, tiled=True)


def laid_out(parts, dim):
    lengths = list(parts.shape[1:])
    lengths[dim] *= parts.shape[0]
    return jnp.moveaxis(parts, 0, dim).reshape(lengths)


def gathered_by_axis(x, axes, dim):
    far, near = axes
    parts = sent_to_all(sent_to_all(x, far), near)
    return laid_out(parts.swapaxes(0, 1).reshape(-1, *x.shape), dim)


def sum_by_parts(x, axes):
    own = sum_in_two_steps(filled_up(x, lax.axis_size(axes[0]) * lax.axis_size(axes[1])), axes, 0)
    whole = gathered_by_axis(own, axes, 0)
    return whole[: len(x)].reshape(x.shape)


def in_one(arrays, axis):
    ends = [0]
    for a in arrays:
        ends.append(ends[-1] + a.size)
    total = sum_by_parts(jnp.concatenate([a.ravel() for a in arrays]), axis)
    return tuple((total[b:e].reshape(a.shape) for a, b, e in zip(arrays, ends, ends[1:])))


def collect(x, axis, dim):
    return laid_out(sent_to_all(x, axis), dim)


def total_of(x, axes):
    padded = filled_up(x, lax.axis_size(axes))
    whole = collect(summed_on_arrival(padded, axes, 0), axes, 0)
    return lax.slice_in_dim(whole, 0, len(x)).reshape(x.shape)


def in_one_2(arrays, axis):
    flat, at, gathered = (jnp.concatenate([a.reshape(-1) for a in arrays]), 0, [])
    total = total_of(flat, axis)
    for a in arrays:
        gathered.append(total[at : at + a.size].reshape(a.shape))
        at += a.size
    return tuple(gathered)


def pair_add(earlier, later):
    return jax.tree.map(lambda left_sum, right_sum: left_sum + right_sum, earlier, later)


def block_pass(
    query_block, key_block, value_block, grad_block, forward_state, backward_state, factor
):
    block_rows = query_block.shape[0]
    causal = (jnp.arange(block_rows)[:, None] >= jnp.arange(block_rows)[None, :])[None]
    attend = jnp.where(
        causal,
        jnp.einsum("thd,shd->hts", query_block, key_block, preferred_element_type=jnp.float32)
        * factor,
        0.0,
    ).astype(jnp.bfloat16)
    pushed = jnp.where(
        causal,
        jnp.einsum("thd,shd->hts", grad_block, value_block, preferred_element_type=jnp.float32)
        * factor,
        0.0,
    ).astype(jnp.bfloat16)
    forward_low = forward_state.astype(jnp.bfloat16)
    backward_low = backward_state.astype(jnp.bfloat16)
    attended = jnp.einsum(
        "hts,shd->thd", attend, value_block, preferred_element_type=jnp.float32
    ) + factor * jnp.einsum(
        "thi,hij->thj", query_block, forward_low, preferred_element_type=jnp.float32
    )
    grad_query = jnp.einsum(
        "hts,shi->thi", pushed, key_block, preferred_element_type=jnp.float32
    ) + factor * jnp.einsum(
        "thj,hij->thi", grad_block, forward_low, preferred_element_type=jnp.float32
    )
    grad_key = jnp.einsum(
        "hts,thi->shi", pushed, query_block, preferred_element_type=jnp.float32
    ) + factor * jnp.einsum(
        "shj,hij->shi", value_block, backward_low, preferred_element_type=jnp.float32
    )
    grad_value = jnp.einsum(
        "hts,thi->shi", attend, grad_block, preferred_element_type=jnp.float32
    ) + factor * jnp.einsum(
        "shi,hij->shj", key_block, backward_low, preferred_element_type=jnp.float32
    )
    return (
        attended.astype(jnp.bfloat16),
        grad_query.astype(jnp.bfloat16),
        grad_key.astype(jnp.bfloat16),
        grad_value.astype(jnp.bfloat16),
    )


def per_device(queries, keys, values, grad_out, lengths):
    tokens_here = queries.shape[1]
    row_width = queries.shape[2]
    row_length = tokens_here * lax.axis_size(SEQ)
    factor = 1.0 / math.sqrt(2.0 * row_length)
    row_index = lax.axis_index(RESP)
    position = lax.axis_index(SEQ) * tokens_here + jnp.arange(tokens_here, dtype=jnp.int32)
    chosen = jnp.arange(lengths.shape[0], dtype=jnp.int32) + 1 == row_index
    limit_tokens = jnp.sum(jnp.where(chosen, lengths, 0)) * BLOCK
    limit_tokens = jnp.where(row_index == 0, row_length, limit_tokens)
    keep_mask = (position < limit_tokens).astype(jnp.bfloat16)[:, None]
    shaped = [
        (array[0] * keep_mask).reshape(tokens_here, HEADS, HEAD)
        for array in (queries, keys, values, grad_out)
    ]
    pieces = [[array for array in shaped]]
    kv_parts = [
        jnp.einsum("thi,thj->hij", piece[1], piece[2], preferred_element_type=jnp.float32)
        for piece in pieces
    ]
    qg_parts = [
        jnp.einsum("thi,thj->hij", piece[0], piece[3], preferred_element_type=jnp.float32)
        for piece in pieces
    ]
    kv_local = sum(kv_parts)
    qg_local = sum(qg_parts)
    zero_state = jnp.zeros_like(kv_local)
    prefix_kv = carried_in(kv_local, SEQ, pair_add, zero_state, False)
    suffix_qg = carried_in(qg_local, SEQ, pair_add, zero_state, True)
    column_kv, column_qg = in_one(
        (jnp.where(row_index == 0, kv_local, 0.0), jnp.where(row_index > 0, qg_local, 0.0)),
        ("resp_0", "resp_1"),
    )
    prompt_state, answer_state = in_one_2((column_kv, column_qg), SEQ)
    forward = jnp.where(row_index == 0, zero_state, prompt_state) + prefix_kv
    backward = jnp.where(row_index == 0, answer_state, zero_state) + suffix_qg
    gathered = [[], [], [], []]
    forward_block = forward + sum(kv_parts[:0])
    backward_block = backward + sum(qg_parts[1:])
    results = block_pass(
        pieces[0][0],
        pieces[0][1],
        pieces[0][2],
        pieces[0][3],
        forward_block,
        backward_block,
        factor,
    )
    for slot in range(4):
        gathered[slot].append(results[slot])
    outputs = [parts[0].reshape(1, tokens_here, row_width) for parts in gathered]
    return (outputs[0], outputs[1], outputs[2], outputs[3])


def solution(mesh):
    finer = Mesh(mesh.devices.reshape(4, 4, 8, 2), ("seq_0", "seq_1", "resp_0", "resp_1"))
    placed = (P(RESP, SEQ, None), P(RESP, SEQ, None), P(RESP, SEQ, None), P(RESP, SEQ, None), P())
    return jax.shard_map(
        per_device,
        mesh=finer,
        in_specs=placed,
        out_specs=(P(RESP, SEQ, None), P(RESP, SEQ, None), P(RESP, SEQ, None), P(RESP, SEQ, None)),
        check_vma=False,
    )
```

profile of v0, /device:TPU:24, one launch (start us, length us, event | category | flops | bytes accessed | tf_op | source)
XLA Modules:
  0.0 206.9 jit_solution(6431296840462511086)
XLA Ops:
  18.7 2.2 %concatenate.17 = f32[4,2,16384]{2,1,0:T(2,128)} reshape(f32[8,128,128]{2,1,0:T(8,128)} %get-tuple-element.20) | data formatting | bytes 1048576 | tf_op jit(solution)/shard_map/concatenate | solution.py:86
  20.8 2.2 %copy.49 = f32[4,2,16384]{2,0,1:T(4,128)} copy(f32[4,2,16384]{2,1,0:T(2,128)} %concatenate.17) | data formatting | bytes 1048576 | tf_op jit(solution)/shard_map/concatenate | solution.py:86
  23.0 2.2 %concatenate.16 = f32[4,2,16384]{2,1,0:T(2,128)} reshape(f32[8,128,128]{2,1,0:T(8,128)} %get-tuple-element.22) | data formatting | bytes 1048576 | tf_op jit(solution)/shard_map/concatenate | solution.py:86
  27.8 5.4 %all_to_all.43 = f32[2,8,16384]{2,1,0:T(8,128)} all-to-all(f32[2,8,16384]{2,1,0:T(8,128)S(1)} %maximum_bitcast_fusion), channel_id=1, replica_groups=mesh['seq_0'=4,'seq_1'=4,'resp_0'=8,'resp_1'=2] {'resp_1'}, dimensions={0} | all-to-all | bytes 2097152 | tf_op jit(solution)/shard_map/all_to_all | solution.py:42
  33.2 2.1 %reduce_sum.37 = f32[8,16384]{1,0:T(8,128)} reduce(f32[2,8,16384]{2,1,0:T(8,128)} %all_to_all.43, f32[]{:T(128)} %constant.37.clone.1), dimensions={0}, to_apply=%region_1.2 | reduce | flops 131072 | bytes 1572868 | tf_op jit(solution)/shard_map/reduce_sum | solution.py:43
  36.8 26.2 %all_to_all.44 = f32[8,1,16384]{2,1,0:T(1,128)} all-to-all(f32[8,1,16384]{2,1,0:T(1,128)S(1)} %all_to_all.29), channel_id=1, replica_groups=mesh['seq_0'=4,'seq_1'=4,'resp_0'=8,'resp_1'=2] {'resp_0'}, dimensions={0} | all-to-all | bytes 1048576 | tf_op jit(solution)/shard_map/all_to_all | solution.py:50
  65.5 4.1 %all-to-all-start.2 = ((f32[8,1,16384]{2,1,0:T(1,128)}), f32[8,1,16384]{2,1,0:T(1,128)}, u32[]{:S(2)}, u32[]{:S(2)}) async-start(f32[8,1,16384]{2,1,0:T(1,128)} %broadcast_in_dim.50), calls=%async_computation.2 | async-start | bytes 1048576 | tf_op jit(solution)/shard_map/all_to_all | solution.py:61
  70.5 4.8 %select_convert_fusion = bf16[8,512,512]{2,1,0:T(8,128)(2,1)} fusion(pred[512,512]{1,0:T(8,128)(4,1)S(1)} %iota_compare_fusion, bf16[512,8,128]{2,1,0:T(8,128)(2,1)} %bitcast.83, bf16[512]{0:T(512)(128)(2,1)S(1)} %fusion.12, bf16[512,8,128]{2,1,0:T(8,128)(2,1)S(1)} %bitcast.75), kind=kOutput, calls=%fused_computation | convolution fusion | flops 544210944 | bytes 6554624 | tf_op jit(solution)/shard_map/thd,shd->hts/dot_general | solution.py:126
  75.3 11.0 %all-to-all-done.2 = f32[8,1,16384]{2,1,0:T(1,128)} async-done(((f32[8,1,16384]{2,1,0:T(1,128)}), f32[8,1,16384]{2,1,0:T(1,128)}, u32[]{:S(2)}, u32[]{:S(2)}) %all-to-all-start.2) | async-done | bytes 524320 | tf_op jit(solution)/shard_map/all_to_all | solution.py:61
  87.8 4.6 %all_to_all.45 = f32[2,8,16384]{2,1,0:T(8,128)S(1)} all-to-all(f32[2,8,16384]{2,1,0:T(8,128)S(1)} %broadcast_in_dim.51), channel_id=1, replica_groups=mesh['seq_0'=4,'seq_1'=4,'resp_0'=8,'resp_1'=2] {'resp_1'}, dimensions={0} | all-to-all | bytes 2097152 | tf_op jit(solution)/shard_map/all_to_all | solution.py:61
  94.5 2.2 %concatenate.19 = f32[8,16384]{1,0:T(8,128)} reshape(f32[4,2,16384]{2,1,0:T(2,128)} %copy.50) | data formatting | bytes 1048576 | tf_op jit(solution)/shard_map/concatenate | solution.py:101
  96.7 2.2 %copy.51 = f32[4,2,16384]{2,1,0:T(2,128)} copy(f32[4,2,16384]{2,0,1:T(4,128)} %get-tuple-element.19) | data formatting | bytes 1048576 | tf_op jit(solution)/shard_map/slice | solution.py:87
  98.9 2.2 %concatenate.20 = f32[8,16384]{1,0:T(8,128)} reshape(f32[4,2,16384]{2,1,0:T(2,128)} %copy.51) | data formatting | bytes 1048576 | tf_op jit(solution)/shard_map/concatenate | solution.py:101
  101.1 2.4 %fusion.5 = f32[1,8,128,128]{3,2,1,0:T(8,128)} fusion(f32[32,128,128]{2,1,0:T(8,128)} %all-gather.13.cloned.1.call-done), kind=kLoop, calls=%fused_computation.24 | loop fusion | flops 393216 | bytes 2621440 | tf_op jit(solution)/shard_map/add | solution.py:110
  104.9 2.0 copy.52
  106.9 7.1 %all-to-all-start.4 = ((f32[16,1,16384]{2,1,0:T(1,128)}), f32[16,1,16384]{2,1,0:T(1,128)}, u32[]{:S(2)}, u32[]{:S(2)}) async-start(f32[16,1,16384]{2,1,0:T(1,128)} %copy.52), calls=%async_computation.4 | async-start | bytes 2097152 | tf_op jit(solution)/shard_map/all_to_all | solution.py:42
  114.0 4.4 %fusion.16 = f32[8,128,512]{2,1,0:T(8,128)} fusion(bf16[8,512,512]{2,1,0:T(8,128)(2,1)} %select_convert_fusion, bf16[512,8,128]{2,1,0:T(8,128)(2,1)S(1)} %bitcast.71, bf16[512]{0:T(512)(128)(2,1)S(1)} %fusion.12), kind=kOutput, calls=%fused_computation.50 | convolution fusion | flops 537395200 | bytes 7341056 | tf_op jit(solution)/shard_map/hts,thi->shi/dot_general | solution.py:142
  118.4 5.2 %fusion.18 = f32[8,128,512]{2,1,0:T(8,128)} fusion(bf16[8,512,512]{2,1,0:T(8,128)(2,1)} %select_convert_fusion, bf16[512,8,128]{2,1,0:T(8,128)(2,1)S(1)} %bitcast.79, bf16[512]{0:T(512)(128)(2,1)S(1)} %fusion.12), kind=kOutput, calls=%fused_computation.52 | convolution fusion | flops 537395200 | bytes 7341056 | tf_op jit(solution)/shard_map/hts,shi->thi/dot_general | solution.py:137
  123.7 3.6 %select_convert_fusion.1 = bf16[8,512,512]{2,1,0:T(8,128)(2,1)} fusion(pred[512,512]{1,0:T(8,128)(4,1)S(1)} %iota_compare_fusion, bf16[512,8,128]{2,1,0:T(8,128)(2,1)S(1)} %bitcast.72, bf16[512]{0:T(512)(128)(2,1)S(1)} %fusion.12, bf16[512,8,128]{2,1,0:T(8,128)(2,1)S(1)} %bitcast.80), kind=kOutput, calls=%fused_computation.1 | convolution fusion | flops 544210944 | bytes 6554624 | tf_op jit(solution)/shard_map/thd,shd->hts/dot_general | solution.py:120
  127.3 6.3 %all-to-all-done.4 = f32[16,1,16384]{2,1,0:T(1,128)} async-done(((f32[16,1,16384]{2,1,0:T(1,128)}), f32[16,1,16384]{2,1,0:T(1,128)}, u32[]{:S(2)}, u32[]{:S(2)}) %all-to-all-start.4) | async-done | bytes 1048608 | tf_op jit(solution)/shard_map/all_to_all | solution.py:42
  137.3 5.7 %all-to-all-start.5 = ((f32[16,1,16384]{2,1,0:T(1,128)}), f32[16,1,16384]{2,1,0:T(1,128)}, u32[]{:S(2)}, u32[]{:S(2)}) async-start(f32[16,1,16384]{2,1,0:T(1,128)} %broadcast_in_dim.52), calls=%async_computation.5 | async-start | bytes 2097152 | tf_op jit(solution)/shard_map/all_to_all | solution.py:61
  143.0 4.5 %fusion.19 = f32[8,128,512]{2,1,0:T(8,128)} fusion(bf16[8,512,512]{2,1,0:T(8,128)(2,1)} %select_convert_fusion.1, bf16[512,8,128]{2,1,0:T(8,128)(2,1)S(1)} %bitcast.76, bf16[512]{0:T(512)(128)(2,1)S(1)} %fusion.12), kind=kOutput, calls=%fused_computation.53 | convolution fusion | flops 537395200 | bytes 7341056 | tf_op jit(solution)/shard_map/hts,thi->shi/dot_general | solution.py:147
  147.6 3.0 %fusion.15 = f32[8,128,512]{2,1,0:T(8,128)} fusion(bf16[8,512,512]{2,1,0:T(8,128)(2,1)S(1)} %copy-done, bf16[512,8,128]{2,1,0:T(8,128)(2,1)S(1)} %bitcast.84, bf16[512]{0:T(512)(128)(2,1)S(1)} %fusion.12), kind=kOutput, calls=%fused_computation.49 | convolution fusion | flops 537395200 | bytes 7341056 | tf_op jit(solution)/shard_map/hts,shd->thd/dot_general | solution.py:132
  150.6 2.4 %fusion.11 = f32[1,8,128,128]{3,2,1,0:T(8,128)} fusion(f32[32,128,128]{2,1,0:T(8,128)} %all-gather.11.cloned.1.call-done), kind=kLoop, calls=%fused_computation.36 | loop fusion | flops 393216 | bytes 2621440 | tf_op jit(solution)/shard_map/add | solution.py:110
  153.0 4.2 %all-to-all-done.5 = f32[16,1,16384]{2,1,0:T(1,128)} async-done(((f32[16,1,16384]{2,1,0:T(1,128)}), f32[16,1,16384]{2,1,0:T(1,128)}, u32[]{:S(2)}, u32[]{:S(2)}) %all-to-all-start.5) | async-done | bytes 1048608 | tf_op jit(solution)/shard_map/all_to_all | solution.py:61
  157.2 3.4 %broadcast_select_fusion = (f32[8,1,16384]{2,1,0:T(1,128)}, f32[8,1,16384]{2,1,0:T(1,128)}) fusion(pred[]{:T(512)S(6)} %eq.12, f32[16,1,16384]{2,1,0:T(1,128)} %all-to-all-done.5), kind=kLoop, calls=%fused_computation.13 | loop fusion | flops 262144 | bytes 2097153 | tf_op jit(solution)/shard_map/jit(_where)/select_n | solution.py:195
  160.6 2.9 %fusion.4 = bf16[8,128,128]{2,1,0:T(8,128)(2,1)S(1)} fusion(f32[8,128,128]{2,1,0:T(8,128)} %bitcast.93, f32[4,8,128,128]{3,2,1,0:T(8,128)} %all-gather.9.cloned.1.call-done, f32[32,128,128]{2,1,0:T(8,128)} %all-gather.13.cloned.1.call-done, pred[]{:T(512)S(6)} %lt.41, pred[]{:T(512)S(6)} %lt.42, pred[]{:T(512)S(6)} %lt.43, pred[]{:T(512)S(6)} %lt.40, ...), kind=kLoop, calls=%fused_computation.20 | loop fusion | flops 2228224 | bytes 4980744 | tf_op jit(solution)/shard_map/convert_element_type | solution.py:131
  165.6 2.3 %copy.60 = bf16[1,512,1024]{2,1,0:T(8,128)(2,1)} copy(bf16[1,512,1024]{1,2,0:T(8,128)(2,1)} %bitcast.88) | data formatting | bytes 2097152
  167.9 20.0 %all-gather.7.cloned.1.call-done = f32[4,8,128,128]{3,2,1,0:T(8,128)} async-done(((f32[1,8,128,128]{3,2,1,0:T(8,128)}), f32[4,8,128,128]{3,2,1,0:T(8,128)}) %all-gather.7.cloned.1.call-update) | async-done | bytes 2097168 | tf_op jit(solution)/shard_map/all_gather | solution.py:25
  187.8 2.9 %fusion.10 = bf16[8,128,128]{2,1,0:T(8,128)(2,1)S(1)} fusion(f32[8,128,128]{2,1,0:T(8,128)} %bitcast.92, f32[4,8,128,128]{3,2,1,0:T(8,128)} %all-gather.7.cloned.1.call-done, f32[32,128,128]{2,1,0:T(8,128)} %all-gather.11.cloned.1.call-done, pred[]{:T(512)S(6)} %gt.33, pred[]{:T(512)S(6)} %gt.34, pred[]{:T(512)S(6)} %gt.35, pred[]{:T(512)S(6)} %gt.32, ...), kind=kLoop, calls=%fused_computation.32 | loop fusion | flops 2228224 | bytes 4980744 | tf_op jit(solution)/shard_map/convert_element_type | solution.py:130
  192.4 2.3 %copy.59 = bf16[1,512,1024]{2,1,0:T(8,128)(2,1)} copy(bf16[1,512,1024]{1,2,0:T(8,128)(2,1)} %bitcast.89) | data formatting | bytes 2097152
  194.7 2.4 %add_convert_fusion.3 = bf16[8,128,512]{2,1,0:T(8,128)(2,1)S(1)} fusion(f32[8,128,512]{2,1,0:T(8,128)} %fusion.15, bf16[8,128,128]{2,1,0:T(8,128)(2,1)} %copy-done.7, bf16[512,8,128]{2,1,0:T(8,128)(2,1)S(1)} %bitcast.73, bf16[512]{0:T(512)(128)(2,1)S(1)} %fusion.12), kind=kOutput, calls=%fused_computation.5 | convolution fusion | flops 136314880 | bytes 4457472 | tf_op jit(solution)/shard_map/thi,hij->thj/dot_general | solution.py:134
  (55 shorter events, 33.9 us)
Async XLA Ops:
  7.2 3.6 %copy-start.8 = (bf16[1,512,1024]{2,1,0:T(8,128)(2,1)S(1)}, bf16[1,512,1024]{2,1,0:T(8,128)(2,1)}, u32[]{:S(2)}) copy-start(bf16[1,512,1024]{2,1,0:T(8,128)(2,1)} %param.8) | copy-start | bytes 3145732
  7.2 94.0 %all-gather.13.cloned.1.call-start = ((), (), s32[]{:S(2)}) async-start(), calls=%async_computation.9 | async-start | bytes 2621440 | tf_op jit(solution)/shard_map/all_gather | solution.py:25
  15.9 1.0 copy-start.1
  65.5 20.8 %all-to-all-start.2 = ((f32[8,1,16384]{2,1,0:T(1,128)}), f32[8,1,16384]{2,1,0:T(1,128)}, u32[]{:S(2)}, u32[]{:S(2)}) async-start(f32[8,1,16384]{2,1,0:T(1,128)} %broadcast_in_dim.50), calls=%async_computation.2 | async-start | bytes 1048576 | tf_op jit(solution)/shard_map/all_to_all | solution.py:61
  69.6 80.9 %all-gather.11.cloned.1.call-start = ((), (), s32[]{:S(2)}) async-start(), calls=%async_computation.8 | async-start | bytes 2621440 | tf_op jit(solution)/shard_map/all_gather | solution.py:25
  70.4 90.3 %all-gather.9.cloned.1.call-start = ((), (), s32[]{:S(2)}) async-start(), calls=%async_computation.7 | async-start | bytes 2621440 | tf_op jit(solution)/shard_map/all_gather | solution.py:25
  106.9 26.7 %all-to-all-start.4 = ((f32[16,1,16384]{2,1,0:T(1,128)}), f32[16,1,16384]{2,1,0:T(1,128)}, u32[]{:S(2)}, u32[]{:S(2)}) async-start(f32[16,1,16384]{2,1,0:T(1,128)} %copy.52), calls=%async_computation.4 | async-start | bytes 2097152 | tf_op jit(solution)/shard_map/all_to_all | solution.py:42
  137.3 19.9 %all-to-all-start.5 = ((f32[16,1,16384]{2,1,0:T(1,128)}), f32[16,1,16384]{2,1,0:T(1,128)}, u32[]{:S(2)}, u32[]{:S(2)}) async-start(f32[16,1,16384]{2,1,0:T(1,128)} %broadcast_in_dim.52), calls=%async_computation.5 | async-start | bytes 2097152 | tf_op jit(solution)/shard_map/all_to_all | solution.py:61
  143.0 44.8 %all-gather.7.cloned.1.call-start = ((), (), s32[]{:S(2)}) async-start(), calls=%async_computation.6 | async-start | bytes 2621440 | tf_op jit(solution)/shard_map/all_gather | solution.py:25
  143.0 4.5 %copy-start = (bf16[8,512,512]{2,1,0:T(8,128)(2,1)S(1)}, bf16[8,512,512]{2,1,0:T(8,128)(2,1)}, u32[]{:S(2)}) copy-start(bf16[8,512,512]{2,1,0:T(8,128)(2,1)} %select_convert_fusion.1) | copy-start | bytes 12582916
  143.0 4.5 %copy-start.2 = (bf16[64,8,8,128]{3,2,1,0:T(8,128)(2,1)S(1)}, bf16[64,8,8,128]{3,2,1,0:T(8,128)(2,1)}, u32[]{:S(2)}) copy-start(bf16[64,8,8,128]{3,2,1,0:T(8,128)(2,1)} %copy-done.1) | copy-start | bytes 3145732
  160.6 2.9 %copy-start.3 = (bf16[64,8,8,128]{3,2,1,0:T(8,128)(2,1)S(1)}, bf16[64,8,8,128]{3,2,1,0:T(8,128)(2,1)}, u32[]{:S(2)}) copy-start(bf16[64,8,8,128]{3,2,1,0:T(8,128)(2,1)} %copy-done.1) | copy-start | bytes 3145732
  160.6 3.3 %copy-start.4 = (f32[8,128,512]{2,1,0:T(8,128)S(1)}, f32[8,128,512]{2,1,0:T(8,128)}, u32[]{:S(2)}) copy-start(f32[8,128,512]{2,1,0:T(8,128)} %fusion.16) | copy-start | bytes 6291460
  187.8 3.0 %copy-start.5 = (f32[8,128,512]{2,1,0:T(8,128)S(1)}, f32[8,128,512]{2,1,0:T(8,128)}, u32[]{:S(2)}) copy-start(f32[8,128,512]{2,1,0:T(8,128)} %fusion.18) | copy-start | bytes 6291460
  190.8 1.6 copy-start.7
  194.7 2.4 %copy-start.6 = (f32[8,128,512]{2,1,0:T(8,128)S(1)}, f32[8,128,512]{2,1,0:T(8,128)}, u32[]{:S(2)}) copy-start(f32[8,128,512]{2,1,0:T(8,128)} %fusion.19) | copy-start | bytes 6291460
Sparse Core Ops, SparseCore 0:
  13.0 34.1 all-gather.12
  72.3 32.8 all-gather.10
  106.9 41.5 all-gather.8
  153.1 34.6 all-gather.6
where the time goes:
time: 209 us; the launch traced here: 207 us
  waiting for transfers between devices  42.2 us (20%)
  local copies, waits for them, and re-layouts  37.9 us (18%)
  blocking collectives  36.1 us (17%)
  matrix products  35.4 us (17%)
  other arithmetic  23.6 us (11%)
  starting transfers between devices  17.1 us (8%)
  between operations  14.6 us (7%)
    all_to_all x1, blocking collectives, sum_in_two_steps(): lax.all_to_all(nearer, far, split_axis=0, concat_axis=0, tiled=True)  26.2 us
    all_gather x4, waiting for transfers between devices, carried_in(): pieces = lax.all_gather(total, axis)  20 us
    all_to_all x2, waiting for transfers between devices, sent_to_all(): return lax.all_to_all(copies, axis, split_axis=0, concat_axis=0, tiled=True)  15.2 us
    unnamed x27, local copies, waits for them, and re-layouts  14.8 us
    all_to_all x2, starting transfers between devices, sent_to_all(): return lax.all_to_all(copies, axis, split_axis=0, concat_axis=0, tiled=True)  9.83 us
    concatenate x4, local copies, waits for them, and re-layouts, in_one(): total = sum_by_parts(jnp.concatenate([a.ravel() for a in arrays]), axis)  7.86 us
    all_to_all x1, starting transfers between devices, summed_on_arrival(): parts = lax.all_to_all(split_up(x, dim, length), axis, 0, 0, tiled=True)  7.1 us
    all_to_all x1, waiting for transfers between devices, summed_on_arrival(): parts = lax.all_to_all(split_up(x, dim, length), axis, 0, 0, tiled=True)  6.3 us
  transfers between devices with their start and end apart: 7, of which 4 were waited for; matrix products, arithmetic and copies ran while one was open for 37% of the time, Pallas kernels for 0%

commit v1 on v0

v1 whole, which is shorter than its diff:
```python
import math

import jax
import jax.numpy as jnp
from jax import lax
from jax.experimental import pallas as pl
from jax.experimental.pallas import tpu as pltpu
from jax.sharding import PartitionSpec as P

HEADS = 8
HEAD = 128
BLOCK = 512
HALF = 256
SEQ = 16
RESP = 16
SHARD = HEADS * HEAD // SEQ
MESH = pl.DeviceIdType.MESH
FACTOR = 1.0 / math.sqrt(2.0 * SEQ * BLOCK)


def dot(a, b, dims):
    return lax.dot_general(a, b, (dims, ((), ())), preferred_element_type=jnp.float32)


NN = ((1,), (0,))
NT = ((1,), (1,))
TN = ((0,), (0,))


def kernel(
    len_ref, k_hbm, v_hbm, q_hbm, g_hbm,
    att_ref, gq_ref, gv_ref, gk_ref,
    x, st, rc, rt, fin, zs, zr, intra,
    in_sem, s1, r1, s2, r2, sz, rz,
):
    me = lax.axis_index("seq")
    row = lax.axis_index("resp")
    fst = (row + RESP - 2) // (RESP - 1)
    snd = 1 - fst

    barrier = pltpu.get_barrier_semaphore()

    def greet(i, _):
        pl.semaphore_signal(barrier, inc=1, device_id=((me + i) % SEQ, row), device_id_type=MESH)
        return 0

    lax.fori_loop(1, SEQ, greet, 0)

    def greet_row(i, _):
        pl.semaphore_signal(barrier, inc=1, device_id=(me, i), device_id_type=MESH)
        return 0

    @pl.when(row == 0)
    def _():
        lax.fori_loop(1, RESP, greet_row, 0)

    @pl.when(row > 0)
    def _():
        greet_row(0, 0)

    sources = (k_hbm, v_hbm, q_hbm, g_hbm)
    for i, source in enumerate(sources):
        pltpu.make_async_copy(source.at[0], x.at[i], in_sem.at[i]).start()

    length = len_ref[fst * (row - 1)]
    keep = jnp.where((row == 0) | (me < length), 1.0, 0.0).astype(jnp.float32)

    def columns(h):
        return pl.ds(pl.multiple_of(h * HEAD, HEAD), HEAD)

    def arrived(i):
        pltpu.make_async_copy(k_hbm.at[0], x.at[i], in_sem.at[i]).wait()

    def to_owner(p, s):
        return pltpu.make_async_remote_copy(
            src_ref=st.at[p, s], dst_ref=rc.at[p, me], send_sem=s1.at[p, s], recv_sem=r1.at[p, me],
            device_id=(s, row), device_id_type=MESH)

    def from_source(p, b):
        return pltpu.make_async_remote_copy(
            src_ref=st.at[p, b], dst_ref=rc.at[p, b], send_sem=s1.at[p, b], recv_sem=r1.at[p, b],
            device_id=(b, row), device_id_type=MESH)

    def to_source(p, b):
        return pltpu.make_async_remote_copy(
            src_ref=rt.at[p, b], dst_ref=fin.at[p, me], send_sem=s2.at[p, b], recv_sem=r2.at[p, me],
            device_id=(b, row), device_id_type=MESH)

    def from_owner(p, s):
        return pltpu.make_async_remote_copy(
            src_ref=rt.at[p, s], dst_ref=fin.at[p, s], send_sem=s2.at[p, s], recv_sem=r2.at[p, s],
            device_id=(s, row), device_id_type=MESH)

    def states(p):
        def one(j, _):
            h = ((me + 1) // 2 + j) % HEADS
            part = dot(x[2 * p, :, columns(h)], x[2 * p + 1, :, columns(h)], TN) * keep
            st[p, pl.ds(2 * h, 2)] = part.reshape(2, SHARD, HEAD)
            for half in range(2):
                @pl.when(2 * h + half != me)
                def _():
                    to_owner(p, 2 * h + half).start()
            return 0

        lax.fori_loop(0, HEADS, one, 0)
        rc[p, me] = st[p, me]

    def inside(h, _):
        c = columns(h)
        k0, k1 = x[0, :HALF, c], x[0, HALF:, c]
        v0, v1 = x[1, :HALF, c], x[1, HALF:, c]
        q0, q1 = x[2, :HALF, c], x[2, HALF:, c]
        g0, g1 = x[3, :HALF, c], x[3, HALF:, c]
        t = lax.broadcasted_iota(jnp.int32, (HALF, HALF), 0)
        s = lax.broadcasted_iota(jnp.int32, (HALF, HALF), 1)
        causal = t >= s

        def triangle(a0, a1, b0, b1):
            d0 = jnp.where(causal, dot(a0, b0, NT) * FACTOR, 0.0).astype(jnp.bfloat16)
            d1 = jnp.where(causal, dot(a1, b1, NT) * FACTOR, 0.0).astype(jnp.bfloat16)
            low = (dot(a1, b0, NT) * FACTOR).astype(jnp.bfloat16)
            return d0, low, d1

        a0, a10, a1 = triangle(q0, q1, k0, k1)
        p0, p10, p1 = triangle(g0, g1, v0, v1)
        intra[0, :HALF, c] = dot(a0, v0, NN)
        intra[0, HALF:, c] = dot(a10, v0, NN) + dot(a1, v1, NN)
        intra[1, :HALF, c] = dot(p0, k0, NN)
        intra[1, HALF:, c] = dot(p10, k0, NN) + dot(p1, k1, NN)
        intra[2, :HALF, c] = dot(a0, g0, TN) + dot(a10, g1, TN)
        intra[2, HALF:, c] = dot(a1, g1, TN)
        intra[3, :HALF, c] = dot(p0, q0, TN) + dot(p10, q1, TN)
        intra[3, HALF:, c] = dot(p1, q1, TN)
        return 0

    def gather_sources(p):
        def one(i, _):
            from_source(p, (me + i) % SEQ).wait_recv()
            return 0

        lax.fori_loop(1, SEQ, one, 0)

    def scanned(p, start):
        def one(i, total):
            b = p * (SEQ - 1) + (1 - 2 * p) * i
            rt[p, b] = total
            return total + rc[p, b]

        return lax.fori_loop(0, SEQ, one, start)

    def give_back(p):
        def one(i, _):
            to_source(p, (me + i) % SEQ).start()
            return 0

        lax.fori_loop(1, SEQ, one, 0)
        fin[p, me] = rt[p, me]

    def total_copy(to, slot):
        return pltpu.make_async_remote_copy(
            src_ref=zs, dst_ref=zr.at[slot], send_sem=sz.at[to], recv_sem=rz.at[slot],
            device_id=(me, to), device_id_type=MESH)

    def finish(p, h, first, second):
        for half in range(2):
            @pl.when(2 * h + half != me)
            def _():
                from_owner(p, 2 * h + half).wait_recv()
        c = columns(h)
        low = fin[p, pl.ds(2 * h, 2)].reshape(HEAD, HEAD).astype(jnp.bfloat16)
        o0, o1, i0, i1 = 2 * p, 2 * p + 1, 2 - 2 * p, 3 - 2 * p
        for o, i, ref, dims in ((o0, i0, first, NN), (o1, i1, second, NT)):
            ref[0, :, c] = ((intra[o, :, c] + FACTOR * dot(x[i, :, c], low, dims)) * keep).astype(jnp.bfloat16)

    def finish_all(p):
        def heads(p, first, second):
            def one(j, _):
                finish(p, ((me + SEQ - 1) // 2 + HEADS - j) % HEADS, first, second)
                return 0

            lax.fori_loop(0, HEADS, one, 0)

        @pl.when(p == 0)
        def _():
            heads(0, att_ref, gq_ref)

        @pl.when(p == 1)
        def _():
            heads(1, gv_ref, gk_ref)

    zero = jnp.zeros((SHARD, HEAD), jnp.float32)

    arrived(2 * fst)
    arrived(2 * fst + 1)

    @pl.when(row == 0)
    def _():
        pl.semaphore_wait(barrier, SEQ + RESP - 2)

    @pl.when(row > 0)
    def _():
        pl.semaphore_wait(barrier, SEQ)

    states(fst)
    arrived(2 * snd)
    arrived(2 * snd + 1)
    states(snd)
    lax.fori_loop(0, HEADS // 2, inside, 0)

    gather_sources(fst)
    zs[...] = scanned(fst, zero)

    @pl.when(row == 0)
    def _():
        def one(i, _):
            total_copy(i, 0).start()
            return 0

        lax.fori_loop(1, RESP, one, 0)

    @pl.when(row > 0)
    def _():
        pltpu.make_async_remote_copy(
            src_ref=zs, dst_ref=zr.at[row], send_sem=sz.at[0], recv_sem=rz.at[row],
            device_id=(me, 0), device_id_type=MESH).start()

    give_back(fst)
    lax.fori_loop(HEADS // 2, HEADS, inside, 0)

    gather_sources(snd)

    @pl.when(row == 0)
    def _():
        def one(i, _):
            total_copy(i, i).wait_recv()
            return 0

        lax.fori_loop(1, RESP, one, 0)
        scanned(snd, lax.fori_loop(1, RESP, lambda i, total: total + zr[i], zero))

    @pl.when(row > 0)
    def _():
        total_copy(0, 0).wait_recv()
        scanned(snd, zr[0])

    give_back(snd)
    finish_all(fst)
    finish_all(snd)

    def sent(i, _):
        for p in range(2):
            to_owner(p, (me + i) % SEQ).wait_send()
            to_source(p, (me + i) % SEQ).wait_send()
        return 0

    lax.fori_loop(1, SEQ, sent, 0)

    @pl.when(row == 0)
    def _():
        def one(i, _):
            total_copy(i, 0).wait_send()
            return 0

        lax.fori_loop(1, RESP, one, 0)

    @pl.when(row > 0)
    def _():
        total_copy(0, 0).wait_send()


def per_device(queries, keys, values, grad_out, lengths):
    shape = queries.shape
    pieces = pltpu.VMEM((2, SEQ, SHARD, HEAD), jnp.float32)
    attended, grad_queries, grad_values, grad_keys = pl.pallas_call(
        kernel,
        out_shape=[jax.ShapeDtypeStruct(shape, jnp.bfloat16)] * 4,
        in_specs=[pl.BlockSpec(memory_space=pltpu.SMEM)] + [pl.BlockSpec(memory_space=pltpu.HBM)] * 4,
        out_specs=[pl.BlockSpec(memory_space=pltpu.VMEM)] * 4,
        scratch_shapes=[
            pltpu.VMEM((4, *shape[1:]), jnp.bfloat16),
            pieces, pieces, pieces, pieces,
            pltpu.VMEM((SHARD, HEAD), jnp.float32),
            pltpu.VMEM((RESP, SHARD, HEAD), jnp.float32),
            pltpu.VMEM((4, *shape[1:]), jnp.float32),
            pltpu.SemaphoreType.DMA((4,)),
            pltpu.SemaphoreType.DMA((2, SEQ)),
            pltpu.SemaphoreType.DMA((2, SEQ)),
            pltpu.SemaphoreType.DMA((2, SEQ)),
            pltpu.SemaphoreType.DMA((2, SEQ)),
            pltpu.SemaphoreType.DMA((RESP,)),
            pltpu.SemaphoreType.DMA((RESP,)),
        ],
        compiler_params=pltpu.CompilerParams(
            collective_id=0, has_side_effects=True, vmem_limit_bytes=49 << 20),
        cost_estimate=pl.CostEstimate(flops=4 << 30, bytes_accessed=8 << 20, transcendentals=0),
        name="lightning",
    )(lengths, keys, values, queries, grad_out)
    return attended, grad_queries, grad_keys, grad_values


def solution(mesh):
    split = P("resp", "seq", None)
    return jax.shard_map(
        per_device,
        mesh=mesh,
        in_specs=(split, split, split, split, P()),
        out_specs=(split, split, split, split),
        check_vma=False,
    )
```

time: 209 us -> 43.2 us (0.21)
  waiting for transfers between devices: 42.2 us -> 0 us
  Pallas kernels: 0 us -> 37.9 us
  blocking collectives: 36.1 us -> 0 us
  matrix products: 35.4 us -> 0 us
  local copies, waits for them, and re-layouts: 37.9 us -> 4.53 us
  other arithmetic: 23.6 us -> 0 us
  starting transfers between devices: 17.1 us -> 0 us
  between operations: 14.6 us -> 0.65 us
    pallas_call x0 -> x1, Pallas kernels: none -> 37.9 us  [per_device(): pl.pallas_call(kernel, out_shape=[jax.ShapeDtypeStruct(shape, jnp.bfloat1...]
    all_to_all x3 -> x0, blocking collectives: 36.1 us -> none  [the longest x1 26.2 us: sum_in_two_steps(): lax.all_to_all(nearer, far, split_axis=0, concat_axis=0, tiled=True)]
    dot_general x12 -> x0, matrix products: 35.4 us -> none  [the longest x1 5.24 us: block_pass(): jnp.einsum('hts,shi->thi', pushed, key_block, preferred_element_type=jnp....]
    all_to_all x3 -> x0, waiting for transfers between devices: 21.5 us -> none  [the longest x2 15.2 us: sent_to_all(): return lax.all_to_all(copies, axis, split_axis=0, concat_axis=0, tiled=True)]
    all_gather x4 -> x0, waiting for transfers between devices: 20 us -> none  [carried_in(): pieces = lax.all_gather(total, axis)]
    all_to_all x3 -> x0, starting transfers between devices: 16.9 us -> none  [the longest x2 9.83 us: sent_to_all(): return lax.all_to_all(copies, axis, split_axis=0, concat_axis=0, tiled=True)]
    concatenate x6 -> x0, local copies, waits for them, and re-layouts: 12.3 us -> none  [the longest x4 7.86 us: in_one(): total = sum_by_parts(jnp.concatenate([a.ravel() for a in arrays]), axis)]
    unnamed x27 -> x6, local copies, waits for them, and re-layouts: 14.8 us -> 4.53 us
  transfers between devices with their start and end apart: 7 -> 0, of which waited for: 4 -> 0; matrix products, arithmetic and copies ran while one was open for 37% -> 0% of each run, Pallas kernels for 0% -> 0%
where the time goes in v1:
time: 43.2 us; the launch traced here: 43.1 us
  Pallas kernels  37.9 us (88%)
  local copies, waits for them, and re-layouts  4.53 us (10%)
  between operations  0.65 us (2%)
    pallas_call x1, Pallas kernels, per_device(): pl.pallas_call(kernel, out_shape=[jax.ShapeDtypeStruct(shape, jnp.bfloat1...  37.9 us
    unnamed x6, local copies, waits for them, and re-layouts  4.53 us

profile of v1, /device:TPU:24, one launch (start us, length us, event | category | flops | bytes accessed | tf_op | source)
XLA Modules:
  0.0 43.1 jit_solution(10849062253547117405)
XLA Ops:
  0.6 0.0 copy-start
  0.6 0.6 %copy-done = s32[15]{0:T(128)S(1)} copy-done((s32[15]{0:T(128)S(1)}, s32[15]{0:T(128)}, u32[]{:S(2)}) %copy-start) | copy-done | bytes 84
  1.3 37.9 %lightning.1 = (bf16[1,512,1024]{2,1,0:T(8,128)(2,1)S(1)}, bf16[1,512,1024]{2,1,0:T(8,128)(2,1)S(1)}, bf16[1,512,1024]{2,1,0:T(8,128)(2,1)S(1)}, bf16[1,512,1024]{2,1,0:T(8,128)(2,1)S(1)}) custom-call(s32[15]{0:T(128)S(1)} %copy-done, bf16[1,512,1024]{2,1,0:T(8,128)(2,1)} %k_hbm.1, bf16[1,512,1024]{2,1,0:T(8,128)(2,1)} %v_hbm.1, ...), custom_call_target="tpu_custom_call" | custom-call | flops 4294967296 | bytes 8388608 | tf_op jit(solution)/shard_map/lightning/pallas_call | solution.py:274
  39.2 1.0 %copy.13 = bf16[1,512,1024]{2,1,0:T(8,128)(2,1)} copy(bf16[1,512,1024]{2,1,0:T(8,128)(2,1)S(1)} %get-tuple-element.16) | data formatting | bytes 2097152
  40.2 1.0 %copy.14 = bf16[1,512,1024]{2,1,0:T(8,128)(2,1)} copy(bf16[1,512,1024]{2,1,0:T(8,128)(2,1)S(1)} %get-tuple-element.17) | data formatting | bytes 2097152
  41.1 1.0 %copy.15 = bf16[1,512,1024]{2,1,0:T(8,128)(2,1)} copy(bf16[1,512,1024]{2,1,0:T(8,128)(2,1)S(1)} %get-tuple-element.18) | data formatting | bytes 2097152
  42.1 1.0 %copy.16 = bf16[1,512,1024]{2,1,0:T(8,128)(2,1)} copy(bf16[1,512,1024]{2,1,0:T(8,128)(2,1)S(1)} %get-tuple-element.19) | data formatting | bytes 2097152
Async XLA Ops:
  0.6 0.7 %copy-start = (s32[15]{0:T(128)S(1)}, s32[15]{0:T(128)}, u32[]{:S(2)}) copy-start(s32[15]{0:T(128)} %len_ref.1) | copy-start | bytes 184

commit v2 on v1

--- a/solution.py
+++ b/solution.py
@@ -266,6 +266,26 @@
     @pl.when(row > 0)
     def _():
         total_copy(0, 0).wait_send()
+
+
+def write_out(*refs):
+    copies = [pltpu.make_async_copy(refs[i], refs[4 + i], refs[8].at[i]) for i in range(4)]
+    for copy in copies:
+        copy.start()
+    for copy in copies:
+        copy.wait()
+
+
+def written(*arrays):
+    return pl.pallas_call(
+        write_out,
+        out_shape=[jax.ShapeDtypeStruct(a.shape, a.dtype) for a in arrays],
+        in_specs=[pl.BlockSpec(memory_space=pltpu.VMEM)] * 4,
+        out_specs=[pl.BlockSpec(memory_space=pl.ANY)] * 4,
+        scratch_shapes=[pltpu.SemaphoreType.DMA((4,))],
+        compiler_params=pltpu.CompilerParams(vmem_limit_bytes=1 << 20),
+        name="write_out",
+    )(*arrays)
 
 
 def per_device(queries, keys, values, grad_out, lengths):
@@ -295,7 +315,7 @@
         cost_estimate=pl.CostEstimate(flops=4 << 30, bytes_accessed=8 << 20, transcendentals=0),
         name="lightning",
     )(lengths, keys, values, queries, grad_out)
-    return attended, grad_queries, grad_keys, grad_values
+    return written(attended, grad_queries, grad_keys, grad_values)
 
 
 def solution(mesh):

time: 43.2 us -> 41.3 us (0.956)
  local copies, waits for them, and re-layouts: 4.53 us -> 0.65 us
  Pallas kernels: 37.9 us -> 39.9 us
    unnamed x6 -> x2, local copies, waits for them, and re-layouts: 4.53 us -> 0.65 us
    pallas_call x0 -> x1, Pallas kernels: none -> 2.04 us  [written(): pl.pallas_call(write_out, out_shape=[jax.ShapeDtypeStruct(a.shape, a.dtyp...]
where the time goes in v2:
time: 41.3 us; the launch traced here: 41.2 us
  Pallas kernels  39.9 us (97%)
  local copies, waits for them, and re-layouts  0.65 us (2%)
  between operations  0.65 us (2%)
    pallas_call x1, Pallas kernels, per_device(): pl.pallas_call(kernel, out_shape=[jax.ShapeDtypeStruct(shape, jnp.bfloat1...  37.9 us
    pallas_call x1, Pallas kernels, written(): pl.pallas_call(write_out, out_shape=[jax.ShapeDtypeStruct(a.shape, a.dtyp...  2.04 us

profile of v2, /device:TPU:24, one launch (start us, length us, event | category | flops | bytes accessed | tf_op | source)
XLA Modules:
  0.0 41.2 jit_solution(5662662589705101499)
XLA Ops:
  0.6 0.0 copy-start
  0.6 0.6 %copy-done = s32[15]{0:T(128)S(1)} copy-done((s32[15]{0:T(128)S(1)}, s32[15]{0:T(128)}, u32[]{:S(2)}) %copy-start) | copy-done | bytes 84
  1.3 37.9 %lightning.1 = (bf16[1,512,1024]{2,1,0:T(8,128)(2,1)S(1)}, bf16[1,512,1024]{2,1,0:T(8,128)(2,1)S(1)}, bf16[1,512,1024]{2,1,0:T(8,128)(2,1)S(1)}, bf16[1,512,1024]{2,1,0:T(8,128)(2,1)S(1)}) custom-call(s32[15]{0:T(128)S(1)} %copy-done, bf16[1,512,1024]{2,1,0:T(8,128)(2,1)} %k_hbm.1, bf16[1,512,1024]{2,1,0:T(8,128)(2,1)} %v_hbm.1, ...), custom_call_target="tpu_custom_call" | custom-call | flops 4294967296 | bytes 8388608 | tf_op jit(solution)/shard_map/lightning/pallas_call | solution.py:294
  39.2 2.0 %write_out.1 = (bf16[1,512,1024]{2,1,0:T(8,128)(2,1)}, bf16[1,512,1024]{2,1,0:T(8,128)(2,1)}, bf16[1,512,1024]{2,1,0:T(8,128)(2,1)}, bf16[1,512,1024]{2,1,0:T(8,128)(2,1)}) custom-call(bf16[1,512,1024]{2,1,0:T(8,128)(2,1)S(1)} %get-tuple-element.8.refs_0_, bf16[1,512,1024]{2,1,0:T(8,128)(2,1)S(1)} %get-tuple-element.9.refs_1_, ...), custom_call_target="tpu_custom_call" | custom-call | tf_op jit(solution)/shard_map/write_out/pallas_call | solution.py:280
Async XLA Ops:
  0.6 0.7 %copy-start = (s32[15]{0:T(128)S(1)}, s32[15]{0:T(128)}, u32[]{:S(2)}) copy-start(s32[15]{0:T(128)} %len_ref.1) | copy-start | bytes 184

commit v3 on v2

--- a/solution.py
+++ b/solution.py
@@ -96,13 +96,16 @@
             h = ((me + 1) // 2 + j) % HEADS
             part = dot(x[2 * p, :, columns(h)], x[2 * p + 1, :, columns(h)], TN) * keep
             st[p, pl.ds(2 * h, 2)] = part.reshape(2, SHARD, HEAD)
-            for half in range(2):
-                @pl.when(2 * h + half != me)
-                def _():
-                    to_owner(p, 2 * h + half).start()
-            return 0
-
-        lax.fori_loop(0, HEADS, one, 0)
+            return 0
+
+        lax.fori_loop(0, HEADS, one, 0, unroll=4)
+
+    def give_out(p):
+        def one(i, _):
+            to_owner(p, (me + i) % SEQ).start()
+            return 0
+
+        lax.fori_loop(1, SEQ, one, 0)
         rc[p, me] = st[p, me]
 
     def inside(h, _):
@@ -178,7 +181,7 @@
                 finish(p, ((me + SEQ - 1) // 2 + HEADS - j) % HEADS, first, second)
                 return 0
 
-            lax.fori_loop(0, HEADS, one, 0)
+            lax.fori_loop(0, HEADS, one, 0, unroll=2)
 
         @pl.when(p == 0)
         def _():
@@ -193,6 +196,8 @@
     arrived(2 * fst)
     arrived(2 * fst + 1)
 
+    states(fst)
+
     @pl.when(row == 0)
     def _():
         pl.semaphore_wait(barrier, SEQ + RESP - 2)
@@ -201,10 +206,11 @@
     def _():
         pl.semaphore_wait(barrier, SEQ)
 
-    states(fst)
+    give_out(fst)
     arrived(2 * snd)
     arrived(2 * snd + 1)
     states(snd)
+    give_out(snd)
     lax.fori_loop(0, HEADS // 2, inside, 0)
 
     gather_sources(fst)

time: 41.3 us -> 40.9 us (level)
  Pallas kernels: 39.9 us -> 39.3 us
    pallas_call x1, Pallas kernels: 37.9 us -> 37.2 us  [per_device(): pl.pallas_call(kernel, out_shape=[jax.ShapeDtypeStruct(shape, jnp.bfloat1...]
where the time goes in v3:
time: 40.9 us; the launch traced here: 40.5 us
  Pallas kernels  39.3 us (96%)
  local copies, waits for them, and re-layouts  0.65 us (2%)
  between operations  0.65 us (2%)
    pallas_call x1, Pallas kernels, per_device(): pl.pallas_call(kernel, out_shape=[jax.ShapeDtypeStruct(shape, jnp.bfloat1...  37.2 us
    pallas_call x1, Pallas kernels, written(): pl.pallas_call(write_out, out_shape=[jax.ShapeDtypeStruct(a.shape, a.dtyp...  2.04 us

profile of v3, /device:TPU:24, one launch (start us, length us, event | category | flops | bytes accessed | tf_op | source)
XLA Modules:
  0.0 40.5 jit_solution(282188838208020096)
XLA Ops:
  0.6 0.0 copy-start
  0.6 0.6 %copy-done = s32[15]{0:T(128)S(1)} copy-done((s32[15]{0:T(128)S(1)}, s32[15]{0:T(128)}, u32[]{:S(2)}) %copy-start) | copy-done | bytes 84
  1.3 37.2 %lightning.1 = (bf16[1,512,1024]{2,1,0:T(8,128)(2,1)S(1)}, bf16[1,512,1024]{2,1,0:T(8,128)(2,1)S(1)}, bf16[1,512,1024]{2,1,0:T(8,128)(2,1)S(1)}, bf16[1,512,1024]{2,1,0:T(8,128)(2,1)S(1)}) custom-call(s32[15]{0:T(128)S(1)} %copy-done, bf16[1,512,1024]{2,1,0:T(8,128)(2,1)} %k_hbm.1, bf16[1,512,1024]{2,1,0:T(8,128)(2,1)} %v_hbm.1, ...), custom_call_target="tpu_custom_call" | custom-call | flops 4294967296 | bytes 8388608 | tf_op jit(solution)/shard_map/lightning/pallas_call | solution.py:300
  38.5 2.0 %write_out.1 = (bf16[1,512,1024]{2,1,0:T(8,128)(2,1)}, bf16[1,512,1024]{2,1,0:T(8,128)(2,1)}, bf16[1,512,1024]{2,1,0:T(8,128)(2,1)}, bf16[1,512,1024]{2,1,0:T(8,128)(2,1)}) custom-call(bf16[1,512,1024]{2,1,0:T(8,128)(2,1)S(1)} %get-tuple-element.8.refs_0_, bf16[1,512,1024]{2,1,0:T(8,128)(2,1)S(1)} %get-tuple-element.9.refs_1_, ...), custom_call_target="tpu_custom_call" | custom-call | tf_op jit(solution)/shard_map/write_out/pallas_call | solution.py:286
Async XLA Ops:
  0.6 0.7 %copy-start = (s32[15]{0:T(128)S(1)}, s32[15]{0:T(128)}, u32[]{:S(2)}) copy-start(s32[15]{0:T(128)} %len_ref.1) | copy-start | bytes 184
